TPU v7x, 32 devices: a whole 2x2x4 slice. The times are simulated.
32 devices in a mesh: section: 8 (over y, x, core), dp: 4 (over z).
Axes of the slice: x: 2, y: 2, z: 4, core: 2. Of those that a mesh axis runs over, the one named last changes fastest.
Arguments:
- pending_adjoints: bfloat16 [2, 8, 4, 16, 32, 256], P(None, 'section', 'dp'), may hold values from -6 to 6
- objective_adjoints: bfloat16 [3, 4, 16, 32, 256], P(None, 'dp'), may hold values from -6 to 6
- kept_block_entries: bfloat16 [2, 8, 4, 4, 16, 32, 256], P(None, 'section', None, 'dp'), may hold values from -6 to 6
- kept_early_presums: bfloat16 [2, 8, 4, 4, 16, 32, 256], P(None, 'section', None, 'dp'), may hold values from -6 to 6
- kept_later_presums: bfloat16 [2, 8, 4, 4, 16, 32, 256], P(None, 'section', None, 'dp'), may hold values from -6 to 6
- filter_taps: bfloat16 [2, 8, 2, 9, 256, 256], P(None, 'section'), may hold values from -0.1875 to 0.1875
- slot_timetable: int32 [4, 16], replicated, may hold values from 0 to 3, as said below
Outputs:
- final_grads: bfloat16 [2, 8, 4, 16, 32, 256], P(None, 'section', 'dp')
- weight_grads: float32 [2, 8, 2, 9, 256, 256], P(None, 'section', None, None, 'dp')
Inputs may be any that keep to these rules, and one draw needn't show every extreme that they name: `slot_timetable`: in each column the slot rises by one from tick to tick, modulo 4, from a starting slot drawn for each section, so each section visits every slot once.
All inputs are finite; a program needn't handle non-finite values.
Results may differ from a plain program's by a relative error of at most 0.017.
Values may be sent and summed in bfloat16 or wider, within the bound.
A program may use at most 192 MiB of HBM per device.

v0:
```python
import functools
import math

import jax
import jax.numpy as jnp
from jax import lax
from jax.experimental import pallas as pl
from jax.experimental.pallas import tpu as pltpu
from jax.sharding import PartitionSpec as P

MESH = pl.DeviceIdType.MESH
LAG = 3


def kernel(
    dims,
    slots,
    pend,
    obj,
    ent,
    pre1,
    pre2,
    taps,
    fin,
    wout,
    cur,
    outg,
    shf,
    act_t,
    own,
    buf_r,
    buf_l,
    enc_s,
    enc_r,
    dec_s,
    dec_r,
    rs,
    rr,
    ls,
    lr,
):
    ticks, levels, replicas, rows, cols, chans, scale = dims
    pix = rows * cols
    share = chans // replicas
    level = lax.axis_index("section")
    rep = lax.axis_index("dp")
    f32, bf16 = jnp.float32, jnp.bfloat16
    has_up, has_down = level < levels - 1, level > 0
    has_right, has_left = rep < replicas - 1, rep > 0

    def hop(src, dst, send, recv, axis, step):
        here = {"section": level, "dp": rep}
        here[axis] = here[axis] + step
        return pltpu.make_async_remote_copy(
            src_ref=src,
            dst_ref=dst,
            send_sem=send,
            recv_sem=recv,
            device_id=(here["section"], here["dp"]),
            device_id_type=MESH,
        )

    barrier = pltpu.get_barrier_semaphore()
    around = (
        (has_up, level + 1, rep),
        (has_down, level - 1, rep),
        (has_right, level, rep + 1),
        (has_left, level, rep - 1),
    )
    for exists, a, b in around:

        @pl.when(exists)
        def _(a=a, b=b):
            pl.semaphore_signal(barrier, inc=1, device_id=(a, b), device_id_type=MESH)

    peers = sum(exists.astype(jnp.int32) for exists, _a, _b in around)
    pl.semaphore_wait(barrier, peers)

    edge = jnp.zeros((cols, chans), bf16)

    def clear(i, carry):
        for h in range(2):
            for c in range(2):
                for d in range(3):
                    shf[h, c, i, d, 0:cols, :] = edge
                    shf[h, c, i, d, cols + pix : 2 * cols + pix, :] = edge
        return carry

    lax.fori_loop(0, ticks, clear, 0)
    column = lax.broadcasted_iota(jnp.int32, (pix, chans), 0) % cols

    def keep(h, c, t, grad):
        wide = grad.astype(f32)
        left = jnp.where(column == 0, 0.0, pltpu.roll(wide, 1, 0))
        right = jnp.where(column == cols - 1, 0.0, pltpu.roll(wide, pix - 1, 0))
        shf[h, c, t, 0, cols : cols + pix, :] = left.astype(bf16)
        shf[h, c, t, 1, cols : cols + pix, :] = grad
        shf[h, c, t, 2, cols : cols + pix, :] = right.astype(bf16)

    def convolve(h, c, t):
        total = None
        for k in range(9):
            piece = lax.dot_general(
                shf[h, c, t, k % 3, (k // 3) * cols : (k // 3) * cols + pix, :],
                taps[h, c, 8 - k],
                (((1,), (1,)), ((), ())),
                preferred_element_type=f32,
            )
            total = piece if total is None else total + piece
        return total

    def slot_of(t, h):
        return slots[t, h * levels + level]

    def upper(h, t, first_tick):
        if first_tick:
            flow = pend[h].astype(f32)
        elif h == 0:
            arrived = cur[t, 0].astype(f32)
            flow = outg[t - 1, 1].astype(f32) + jnp.where(has_up, arrived, 0.0)
        else:
            flow = jnp.where(has_down, cur[t, 1], obj[t - 1]).astype(f32)
        later = pre2[h, slot_of(t, h)].astype(f32)
        keep(h, 1, t, jnp.where(later > 0, flow, 0.0).astype(bf16))

    def lower(h, t):
        early = pre1[h, slot_of(t, h)].astype(f32)
        keep(h, 0, t, jnp.where(early > 0, convolve(h, 1, t), 0.0).astype(bf16))
        outg[t, h] = convolve(h, 0, t).astype(bf16)

    def enc_hop(t):
        return hop(outg.at[t, 0], cur.at[t + 1, 0], enc_s.at[t], enc_r.at[t], "section", -1)

    def dec_hop(t):
        return hop(outg.at[t, 1], cur.at[t + 1, 1], dec_s.at[t], dec_r.at[t], "section", 1)

    def send(t):
        @pl.when(has_up)
        def _():
            dec_hop(t).start()

    def send_enc(t):
        @pl.when(has_down)
        def _():
            enc_hop(t).start()

    def arrive_dec(t):
        @pl.when(has_down)
        def _():
            dec_hop(t - 1).wait_recv()

    def arrive_enc(t):
        @pl.when(has_up)
        def _():
            enc_hop(t - 1).wait_recv()

    def turn(t):
        for h in range(2):
            place = pl.ds(pl.multiple_of(t * pix, pix), pix)
            act_t[h, 0, :, place] = ent[h, slot_of(t, h)].T
            early = pre1[h, slot_of(t, h)]
            act_t[h, 1, :, place] = jnp.maximum(early, jnp.zeros_like(early)).T

    upper(1, 0, True)
    lower(1, 0)
    send(0)
    upper(0, 0, True)
    lower(0, 0)
    send_enc(0)
    turn(0)

    def tick(t, carry):
        arrive_dec(t)
        upper(1, t, False)
        lower(1, t)
        send(t)
        arrive_enc(t)
        upper(0, t, False)
        lower(0, t)
        send_enc(t)
        turn(t)
        return carry

    lax.fori_loop(1, ticks - 1, tick, 0)
    final = ticks - 1
    turn(final)
    arrive_dec(final)
    upper(1, final, False)
    arrive_enc(final)
    upper(0, final, False)

    def right_hop(u, j):
        return hop(buf_r.at[u, j], buf_r.at[u, j], rs.at[u, j], rr.at[u, j], "dp", 1)

    def left_hop(u, j):
        return hop(buf_l.at[u, j], buf_l.at[u, j], ls.at[u, j], lr.at[u, j], "dp", -1)

    def unit(c, u):
        h, a = (u % 6) // 3, u % 3
        start = pl.multiple_of((2 - a) * cols, cols)
        left = act_t[h, c]
        for i in range(3):
            right = jnp.concatenate(
                [shf[h, c, t, 2 - i, pl.ds(start, pix), :] for t in range(ticks)], axis=0
            )
            own[u % (LAG + 1), :, i * chans : (i + 1) * chans] = jnp.dot(
                left, right, preferred_element_type=f32
            )

    def mine(u, j):
        return own[u % (LAG + 1), j * share : (j + 1) * share, :]

    def lead(u):
        for j in reversed(range(1, replicas)):

            @pl.when(rep == 0)
            def _(j=j):
                buf_r[u, j] = mine(u, j).astype(bf16)
                right_hop(u, j).start()

        for j in range(replicas - 1):

            @pl.when(rep == replicas - 1)
            def _(j=j):
                buf_l[u, j] = mine(u, j).astype(bf16)
                left_hop(u, j).start()

    def relay(u):
        for j in reversed(range(1, replicas)):

            @pl.when(has_left & (rep < j))
            def _(j=j):
                right_hop(u, j).wait_recv()
                buf_r[u, j] = (mine(u, j) + buf_r[u, j].astype(f32)).astype(bf16)
                right_hop(u, j).start()

        for j in range(replicas - 1):

            @pl.when(has_right & (rep > j))
            def _(j=j):
                left_hop(u, j).wait_recv()
                buf_l[u, j] = (mine(u, j) + buf_l[u, j].astype(f32)).astype(bf16)
                left_hop(u, j).start()

        c, h, a = 1 - u // 6, (u % 6) // 3, u % 3
        for j in range(replicas):

            @pl.when(rep == j)
            def _(j=j):
                total = mine(u, j)
                if j > 0:
                    right_hop(u, j).wait_recv()
                    total = total + buf_r[u, j].astype(f32)
                if j < replicas - 1:
                    left_hop(u, j).wait_recv()
                    total = total + buf_l[u, j].astype(f32)
                total = total * scale
                for i in range(3):
                    wout[h, c, a * 3 + i] = total[:, i * chans : (i + 1) * chans]

    def first_half(u, carry):
        unit(1, u)
        lead(u)

        @pl.when(u >= LAG)
        def _():
            relay(u - LAG)

        return carry

    lax.fori_loop(0, 6, first_half, 0)
    for h in range(2):
        lower(h, final)
        fin[h] = outg[final, h]

    def second_half(u, carry):
        unit(0, u)
        lead(u)
        relay(u - LAG)
        return carry

    lax.fori_loop(6, 12, second_half, 0)

    def rest(u, carry):
        relay(u)
        return carry

    lax.fori_loop(12 - LAG, 12, rest, 0)

    def drain(u, carry):
        for j in range(replicas):

            @pl.when(rep < j)
            def _(j=j):
                right_hop(u, j).wait_send()

            @pl.when(rep > j)
            def _(j=j):
                left_hop(u, j).wait_send()

        return carry

    lax.fori_loop(0, 12, drain, 0)

    def drain_chain(t, carry):
        @pl.when(has_up)
        def _():
            dec_hop(t).wait_send()

        @pl.when(has_down)
        def _():
            enc_hop(t).wait_send()

        return carry

    lax.fori_loop(0, ticks - 1, drain_chain, 0)


def on_device(pending, objective, entries, early, later, taps, slots):
    levels = lax.axis_size("section")
    replicas = lax.axis_size("dp")
    images, rows, cols, chans = pending.shape[2:]
    ticks = slots.shape[0]
    kept = entries.shape[2]
    pix = images * rows * cols
    scale = 1.0 / math.sqrt(ticks * replicas * pix)
    dims = (ticks, levels, replicas, rows, cols, chans, scale)
    bf16 = jnp.bfloat16
    share = chans // replicas
    whole = pl.BlockSpec(memory_space=pltpu.VMEM)
    dma = pltpu.SemaphoreType.DMA
    fin, wout = pl.pallas_call(
        functools.partial(kernel, dims),
        out_shape=(
            jax.ShapeDtypeStruct((2, pix, chans), bf16),
            jax.ShapeDtypeStruct((2, 2, 9, share, chans), jnp.float32),
        ),
        in_specs=[pl.BlockSpec(memory_space=pltpu.SMEM)] + [whole] * 6,
        out_specs=(whole, whole),
        scratch_shapes=[
            pltpu.VMEM((ticks, 2, pix, chans), bf16),
            pltpu.VMEM((ticks, 2, pix, chans), bf16),
            pltpu.VMEM((2, 2, ticks, 3, pix + 2 * cols, chans), bf16),
            pltpu.VMEM((2, 2, chans, ticks * pix), bf16),
            pltpu.VMEM((LAG + 1, chans, 3 * chans), jnp.float32),
            pltpu.VMEM((12, replicas, share, 3 * chans), bf16),
            pltpu.VMEM((12, replicas, share, 3 * chans), bf16),
            dma((ticks - 1,)),
            dma((ticks - 1,)),
            dma((ticks - 1,)),
            dma((ticks - 1,)),
            dma((12, replicas)),
            dma((12, replicas)),
            dma((12, replicas)),
            dma((12, replicas)),
        ],
        compiler_params=pltpu.CompilerParams(
            collective_id=0, has_side_effects=True, vmem_limit_bytes=67043328
        ),
    )(
        slots,
        pending.reshape(2, pix, chans),
        objective.reshape(-1, pix, chans),
        entries.reshape(2, kept, pix, chans),
        early.reshape(2, kept, pix, chans),
        later.reshape(2, kept, pix, chans),
        taps.reshape(2, 2, 9, chans, chans),
    )
    return (
        fin.reshape(2, 1, images, rows, cols, chans),
        wout.reshape(2, 1, 2, 9, share, chans),
    )


def solution(mesh):
    placed = (
        P(None, "section", "dp", None, None, None),
        P(None, "dp", None, None, None),
        P(None, "section", None, "dp", None, None, None),
        P(None, "section", None, "dp", None, None, None),
        P(None, "section", None, "dp", None, None, None),
        P(None, "section", None, None, None, None),
        P(),
    )
    return jax.shard_map(
        on_device,
        mesh=mesh,
        in_specs=placed,
        out_specs=(
            P(None, "section", "dp", None, None, None),
            P(None, "section", None, None, "dp", None),
        ),
        check_vma=False,
    )
```

profile of v0, /device:TPU:4, one launch (start us, length us, event | category | flops | bytes accessed | tf_op | source)
XLA Modules:
  0.0 167.5 jit_solution(18406086471797903737)
XLA Ops:
  0.6 161.7 %shard_map.86 = (bf16[2,512,256]{2,1,0:T(8,128)(2,1)}, f32[2,2,9,64,256]{4,3,2,1,0:T(8,128)}) custom-call(s32[4,16]{1,0:T(4,128)} %slots.1, bf16[2,512,256]{2,1,0:T(8,128)(2,1)} %bitcast.18, bf16[3,512,256]{2,1,0:T(8,128)(2,1)} %bitcast.17, bf16[2,4,512,256]{3,2,1,0:T(8,128)(2,1)} %bitcast.14, bf16[2,4,512,256]{3,2,1,0:T(8,128)(2,1)} %bitcast.15, ...), custom_call_target="tpu_custom_call" | custom-call | tf_op jit(solution)/shard_map/pallas_call | solution.py:332
  162.4 1.9 %copy.13 = bf16[2,1,1,16,32,256]{5,4,3,2,1,0:T(8,128)(2,1)} copy(bf16[2,1,1,16,32,256]{5,4,3,2,1,0:T(8,128)(2,1)} %bitcast.19) | data formatting | bytes 1048576
  164.2 3.3 %copy.14 = f32[2,1,2,9,64,256]{5,4,3,2,1,0:T(8,128)} copy(f32[2,1,2,9,64,256]{5,4,3,2,1,0:T(8,128)} %bitcast.13) | data formatting | bytes 4718592
where the time goes:
time: 169 us; the launch traced here: 168 us
  Pallas kernels  162 us (96%)
  local copies, waits for them, and re-layouts  5.19 us (3%)
    pallas_call x1, Pallas kernels, on_device(): pl.pallas_call(functools.partial(kernel, dims), out_shape=(jax.ShapeDtype...  162 us
    unnamed x2, local copies, waits for them, and re-layouts  5.19 us

commit v1 on v0

--- a/solution.py
+++ b/solution.py
@@ -17,12 +17,15 @@
     slots,
     pend,
     obj,
-    ent,
     pre1,
     pre2,
-    taps,
+    ent_in,
+    taps_in,
     fin,
     wout,
+    ent,
+    taps,
+    loaded,
     cur,
     outg,
     shf,
@@ -60,6 +63,18 @@
             device_id_type=MESH,
         )
 
+    def fetch(h, c):
+        return pltpu.make_async_copy(taps_in.at[h, c], taps.at[h, c], loaded.at[h, c])
+
+    def fetch_entries():
+        return pltpu.make_async_copy(ent_in, ent, loaded.at[2, 0])
+
+    fetch(1, 1).start()
+    fetch(1, 0).start()
+    fetch(0, 1).start()
+    fetch(0, 0).start()
+    fetch_entries().start()
+
     barrier = pltpu.get_barrier_semaphore()
     around = (
         (has_up, level + 1, rep),
@@ -98,16 +113,17 @@
         shf[h, c, t, 2, cols : cols + pix, :] = right.astype(bf16)
 
     def convolve(h, c, t):
-        total = None
-        for k in range(9):
-            piece = lax.dot_general(
-                shf[h, c, t, k % 3, (k // 3) * cols : (k // 3) * cols + pix, :],
-                taps[h, c, 8 - k],
-                (((1,), (1,)), ((), ())),
-                preferred_element_type=f32,
-            )
-            total = piece if total is None else total + piece
-        return total
+        wide = jnp.concatenate(
+            [
+                shf[h, c, t, k % 3, (k // 3) * cols : (k // 3) * cols + pix, :]
+                for k in range(9)
+            ],
+            axis=1,
+        )
+        filt = jnp.concatenate([taps[h, c, 8 - k] for k in range(9)], axis=1)
+        return lax.dot_general(
+            wide, filt, (((1,), (1,)), ((), ())), preferred_element_type=f32
+        )
 
     def slot_of(t, h):
         return slots[t, h * levels + level]
@@ -154,20 +170,32 @@
         def _():
             enc_hop(t - 1).wait_recv()
 
-    def turn(t):
-        for h in range(2):
-            place = pl.ds(pl.multiple_of(t * pix, pix), pix)
+    def turn(h, c, t):
+        place = pl.ds(pl.multiple_of(t * pix, pix), pix)
+        if c == 0:
             act_t[h, 0, :, place] = ent[h, slot_of(t, h)].T
+        else:
             early = pre1[h, slot_of(t, h)]
             act_t[h, 1, :, place] = jnp.maximum(early, jnp.zeros_like(early)).T
 
+    def turn_all(h, c):
+        def one(t, carry):
+            turn(h, c, t)
+            return carry
+
+        lax.fori_loop(0, ticks, one, 0)
+
     upper(1, 0, True)
+    fetch(1, 1).wait()
+    fetch(1, 0).wait()
     lower(1, 0)
     send(0)
     upper(0, 0, True)
+    fetch(0, 1).wait()
+    fetch(0, 0).wait()
     lower(0, 0)
     send_enc(0)
-    turn(0)
+    turn(1, 1, 0)
 
     def tick(t, carry):
         arrive_dec(t)
@@ -178,16 +206,14 @@
         upper(0, t, False)
         lower(0, t)
         send_enc(t)
-        turn(t)
+        turn(1, 1, t)
         return carry
 
     lax.fori_loop(1, ticks - 1, tick, 0)
     final = ticks - 1
-    turn(final)
+    turn(1, 1, final)
     arrive_dec(final)
     upper(1, final, False)
-    arrive_enc(final)
-    upper(0, final, False)
 
     def right_hop(u, j):
         return hop(buf_r.at[u, j], buf_r.at[u, j], rs.at[u, j], rr.at[u, j], "dp", 1)
@@ -195,20 +221,20 @@
     def left_hop(u, j):
         return hop(buf_l.at[u, j], buf_l.at[u, j], ls.at[u, j], lr.at[u, j], "dp", -1)
 
-    def unit(c, u):
-        h, a = (u % 6) // 3, u % 3
+    def unit(h, c, u):
+        a = u % 3
         start = pl.multiple_of((2 - a) * cols, cols)
         left = act_t[h, c]
         for i in range(3):
             right = jnp.concatenate(
                 [shf[h, c, t, 2 - i, pl.ds(start, pix), :] for t in range(ticks)], axis=0
             )
-            own[u % (LAG + 1), :, i * chans : (i + 1) * chans] = jnp.dot(
+            own[u % (LAG + 2), :, i * chans : (i + 1) * chans] = jnp.dot(
                 left, right, preferred_element_type=f32
             )
 
     def mine(u, j):
-        return own[u % (LAG + 1), j * share : (j + 1) * share, :]
+        return own[u % (LAG + 2), j * share : (j + 1) * share, :]
 
     def lead(u):
         for j in reversed(range(1, replicas)):
@@ -225,7 +251,7 @@
                 buf_l[u, j] = mine(u, j).astype(bf16)
                 left_hop(u, j).start()
 
-    def relay(u):
+    def relay_right(u):
         for j in reversed(range(1, replicas)):
 
             @pl.when(has_left & (rep < j))
@@ -234,6 +260,7 @@
                 buf_r[u, j] = (mine(u, j) + buf_r[u, j].astype(f32)).astype(bf16)
                 right_hop(u, j).start()
 
+    def relay_left(u):
         for j in range(replicas - 1):
 
             @pl.when(has_right & (rep > j))
@@ -242,7 +269,28 @@
                 buf_l[u, j] = (mine(u, j) + buf_l[u, j].astype(f32)).astype(bf16)
                 left_hop(u, j).start()
 
-        c, h, a = 1 - u // 6, (u % 6) // 3, u % 3
+    near_left = rep * 2 < replicas
+
+    def relay_near(u):
+        @pl.when(near_left)
+        def _():
+            relay_right(u)
+
+        @pl.when(jnp.logical_not(near_left))
+        def _():
+            relay_left(u)
+
+    def relay_far(u):
+        @pl.when(near_left)
+        def _():
+            relay_left(u)
+
+        @pl.when(jnp.logical_not(near_left))
+        def _():
+            relay_right(u)
+
+    def finish(u):
+        c, h, a = 1 - u // 6, 1 - (u // 3) % 2, u % 3
         for j in range(replicas):
 
             @pl.when(rep == j)
@@ -258,34 +306,45 @@
                 for i in range(3):
                     wout[h, c, a * 3 + i] = total[:, i * chans : (i + 1) * chans]
 
-    def first_half(u, carry):
-        unit(1, u)
-        lead(u)
-
-        @pl.when(u >= LAG)
-        def _():
-            relay(u - LAG)
-
+    def advance(u):
+        @pl.when((u >= LAG) & (u < 12 + LAG))
+        def _():
+            relay_near(u - LAG)
+
+        @pl.when(u > LAG)
+        def _():
+            relay_far(u - LAG - 1)
+            finish(u - LAG - 1)
+
+    def group(g):
+        def one(u, carry):
+            unit(1 - g % 2, 1 - g // 2, u)
+            lead(u)
+            advance(u)
+            return carry
+
+        lax.fori_loop(3 * g, 3 * g + 3, one, 0)
+
+    group(0)
+    turn_all(0, 1)
+    fetch_entries().wait()
+    arrive_enc(final)
+    upper(0, final, False)
+    group(1)
+    turn_all(1, 0)
+    lower(1, final)
+    fin[1] = outg[final, 1]
+    group(2)
+    turn_all(0, 0)
+    lower(0, final)
+    fin[0] = outg[final, 0]
+    group(3)
+
+    def rest(u, carry):
+        advance(u)
         return carry
 
-    lax.fori_loop(0, 6, first_half, 0)
-    for h in range(2):
-        lower(h, final)
-        fin[h] = outg[final, h]
-
-    def second_half(u, carry):
-        unit(0, u)
-        lead(u)
-        relay(u - LAG)
-        return carry
-
-    lax.fori_loop(6, 12, second_half, 0)
-
-    def rest(u, carry):
-        relay(u)
-        return carry
-
-    lax.fori_loop(12 - LAG, 12, rest, 0)
+    lax.fori_loop(12, 13 + LAG, rest, 0)
 
     def drain(u, carry):
         for j in range(replicas):
@@ -328,6 +387,7 @@
     bf16 = jnp.bfloat16
     share = chans // replicas
     whole = pl.BlockSpec(memory_space=pltpu.VMEM)
+    anywhere = pl.BlockSpec(memory_space=pl.ANY)
     dma = pltpu.SemaphoreType.DMA
     fin, wout = pl.pallas_call(
         functools.partial(kernel, dims),
@@ -335,14 +395,17 @@
             jax.ShapeDtypeStruct((2, pix, chans), bf16),
             jax.ShapeDtypeStruct((2, 2, 9, share, chans), jnp.float32),
         ),
-        in_specs=[pl.BlockSpec(memory_space=pltpu.SMEM)] + [whole] * 6,
+        in_specs=[pl.BlockSpec(memory_space=pltpu.SMEM)] + [whole] * 4 + [anywhere] * 2,
         out_specs=(whole, whole),
         scratch_shapes=[
+            pltpu.VMEM((2, kept, pix, chans), bf16),
+            pltpu.VMEM((2, 2, 9, chans, chans), bf16),
+            dma((3, 2)),
             pltpu.VMEM((ticks, 2, pix, chans), bf16),
             pltpu.VMEM((ticks, 2, pix, chans), bf16),
             pltpu.VMEM((2, 2, ticks, 3, pix + 2 * cols, chans), bf16),
             pltpu.VMEM((2, 2, chans, ticks * pix), bf16),
-            pltpu.VMEM((LAG + 1, chans, 3 * chans), jnp.float32),
+            pltpu.VMEM((LAG + 2, chans, 3 * chans), jnp.float32),
             pltpu.VMEM((12, replicas, share, 3 * chans), bf16),
             pltpu.VMEM((12, replicas, share, 3 * chans), bf16),
             dma((ticks - 1,)),
@@ -361,9 +424,9 @@
         slots,
         pending.reshape(2, pix, chans),
         objective.reshape(-1, pix, chans),
-        entries.reshape(2, kept, pix, chans),
         early.reshape(2, kept, pix, chans),
         later.reshape(2, kept, pix, chans),
+        entries.reshape(2, kept, pix, chans),
         taps.reshape(2, 2, 9, chans, chans),
     )
     return (

time: 169 us -> 121 us (0.72)
  Pallas kernels: 162 us -> 115 us
    pallas_call x1, Pallas kernels: 162 us -> 115 us  [on_device(): pl.pallas_call(functools.partial(kernel, dims), out_shape=(jax.ShapeDtype...]
where the time goes in v1:
time: 121 us
  Pallas kernels  115 us (95%)
  local copies, waits for them, and re-layouts  5.19 us (4%)
    pallas_call x1, Pallas kernels, on_device(): pl.pallas_call(functools.partial(kernel, dims), out_shape=(jax.ShapeDtype...  115 us
    unnamed x2, local copies, waits for them, and re-layouts  5.19 us

profile of v1, /device:TPU:4, one launch (start us, length us, event | category | flops | bytes accessed | tf_op | source)
XLA Modules:
  0.0 121.1 jit_solution(12118973562555505174)
XLA Ops:
  0.6 115.2 %shard_map.86 = (bf16[2,512,256]{2,1,0:T(8,128)(2,1)}, f32[2,2,9,64,256]{4,3,2,1,0:T(8,128)}) custom-call(s32[4,16]{1,0:T(4,128)} %slots.1, bf16[2,512,256]{2,1,0:T(8,128)(2,1)} %bitcast.18, bf16[3,512,256]{2,1,0:T(8,128)(2,1)} %bitcast.17, bf16[2,4,512,256]{3,2,1,0:T(8,128)(2,1)} %bitcast.14, bf16[2,4,512,256]{3,2,1,0:T(8,128)(2,1)} %bitcast.15, ...), custom_call_target="tpu_custom_call" | custom-call | tf_op jit(solution)/shard_map/pallas_call | solution.py:392
  115.9 1.9 %copy.13 = bf16[2,1,1,16,32,256]{5,4,3,2,1,0:T(8,128)(2,1)} copy(bf16[2,1,1,16,32,256]{5,4,3,2,1,0:T(8,128)(2,1)} %bitcast.19) | data formatting | bytes 1048576
  117.8 3.3 %copy.14 = f32[2,1,2,9,64,256]{5,4,3,2,1,0:T(8,128)} copy(f32[2,1,2,9,64,256]{5,4,3,2,1,0:T(8,128)} %bitcast.13) | data formatting | bytes 4718592

commit v2 on v1

--- a/solution.py
+++ b/solution.py
@@ -16,13 +16,15 @@
     dims,
     slots,
     pend,
-    obj,
-    pre1,
     pre2,
+    obj_in,
+    pre1_in,
     ent_in,
     taps_in,
     fin,
     wout,
+    obj,
+    pre1,
     ent,
     taps,
     loaded,
@@ -42,7 +44,7 @@
     ls,
     lr,
 ):
-    ticks, levels, replicas, rows, cols, chans, scale = dims
+    ticks, levels, replicas, rows, cols, chans = dims
     pix = rows * cols
     share = chans // replicas
     level = lax.axis_index("section")
@@ -66,13 +68,21 @@
     def fetch(h, c):
         return pltpu.make_async_copy(taps_in.at[h, c], taps.at[h, c], loaded.at[h, c])
 
+    def fetch_early():
+        return pltpu.make_async_copy(pre1_in, pre1, loaded.at[2, 1])
+
+    def fetch_objective():
+        return pltpu.make_async_copy(obj_in, obj, loaded.at[3, 0])
+
     def fetch_entries():
         return pltpu.make_async_copy(ent_in, ent, loaded.at[2, 0])
 
     fetch(1, 1).start()
+    fetch_early().start()
     fetch(1, 0).start()
     fetch(0, 1).start()
     fetch(0, 0).start()
+    fetch_objective().start()
     fetch_entries().start()
 
     barrier = pltpu.get_barrier_semaphore()
@@ -89,7 +99,6 @@
             pl.semaphore_signal(barrier, inc=1, device_id=(a, b), device_id_type=MESH)
 
     peers = sum(exists.astype(jnp.int32) for exists, _a, _b in around)
-    pl.semaphore_wait(barrier, peers)
 
     edge = jnp.zeros((cols, chans), bf16)
 
@@ -113,17 +122,23 @@
         shf[h, c, t, 2, cols : cols + pix, :] = right.astype(bf16)
 
     def convolve(h, c, t):
-        wide = jnp.concatenate(
-            [
-                shf[h, c, t, k % 3, (k // 3) * cols : (k // 3) * cols + pix, :]
-                for k in range(9)
-            ],
-            axis=1,
-        )
         filt = jnp.concatenate([taps[h, c, 8 - k] for k in range(9)], axis=1)
-        return lax.dot_general(
-            wide, filt, (((1,), (1,)), ((), ())), preferred_element_type=f32
-        )
+        half = pix // 2
+        parts = []
+        for lo in (0, half):
+            wide = jnp.concatenate(
+                [
+                    shf[h, c, t, k % 3, (k // 3) * cols + lo : (k // 3) * cols + lo + half, :]
+                    for k in range(9)
+                ],
+                axis=1,
+            )
+            parts.append(
+                lax.dot_general(
+                    wide, filt, (((1,), (1,)), ((), ())), preferred_element_type=f32
+                )
+            )
+        return jnp.concatenate(parts, axis=0)
 
     def slot_of(t, h):
         return slots[t, h * levels + level]
@@ -187,8 +202,10 @@
 
     upper(1, 0, True)
     fetch(1, 1).wait()
+    fetch_early().wait()
     fetch(1, 0).wait()
     lower(1, 0)
+    pl.semaphore_wait(barrier, peers)
     send(0)
     upper(0, 0, True)
     fetch(0, 1).wait()
@@ -196,6 +213,8 @@
     lower(0, 0)
     send_enc(0)
     turn(1, 1, 0)
+
+    fetch_objective().wait()
 
     def tick(t, carry):
         arrive_dec(t)
@@ -302,9 +321,8 @@
                 if j < replicas - 1:
                     left_hop(u, j).wait_recv()
                     total = total + buf_l[u, j].astype(f32)
-                total = total * scale
                 for i in range(3):
-                    wout[h, c, a * 3 + i] = total[:, i * chans : (i + 1) * chans]
+                    wout[h, c, a * 3 + i] = total[:, i * chans : (i + 1) * chans].astype(bf16)
 
     def advance(u):
         @pl.when((u >= LAG) & (u < 12 + LAG))
@@ -383,7 +401,7 @@
     kept = entries.shape[2]
     pix = images * rows * cols
     scale = 1.0 / math.sqrt(ticks * replicas * pix)
-    dims = (ticks, levels, replicas, rows, cols, chans, scale)
+    dims = (ticks, levels, replicas, rows, cols, chans)
     bf16 = jnp.bfloat16
     share = chans // replicas
     whole = pl.BlockSpec(memory_space=pltpu.VMEM)
@@ -393,14 +411,16 @@
         functools.partial(kernel, dims),
         out_shape=(
             jax.ShapeDtypeStruct((2, pix, chans), bf16),
-            jax.ShapeDtypeStruct((2, 2, 9, share, chans), jnp.float32),
+            jax.ShapeDtypeStruct((2, 2, 9, share, chans), bf16),
         ),
-        in_specs=[pl.BlockSpec(memory_space=pltpu.SMEM)] + [whole] * 4 + [anywhere] * 2,
+        in_specs=[pl.BlockSpec(memory_space=pltpu.SMEM)] + [whole] * 2 + [anywhere] * 4,
         out_specs=(whole, whole),
         scratch_shapes=[
+            pltpu.VMEM((ticks - 1, pix, chans), bf16),
+            pltpu.VMEM((2, kept, pix, chans), bf16),
             pltpu.VMEM((2, kept, pix, chans), bf16),
             pltpu.VMEM((2, 2, 9, chans, chans), bf16),
-            dma((3, 2)),
+            dma((4, 2)),
             pltpu.VMEM((ticks, 2, pix, chans), bf16),
             pltpu.VMEM((ticks, 2, pix, chans), bf16),
             pltpu.VMEM((2, 2, ticks, 3, pix + 2 * cols, chans), bf16),
@@ -423,15 +443,15 @@
     )(
         slots,
         pending.reshape(2, pix, chans),
+        later.reshape(2, kept, pix, chans),
         objective.reshape(-1, pix, chans),
         early.reshape(2, kept, pix, chans),
-        later.reshape(2, kept, pix, chans),
         entries.reshape(2, kept, pix, chans),
         taps.reshape(2, 2, 9, chans, chans),
     )
     return (
         fin.reshape(2, 1, images, rows, cols, chans),
-        wout.reshape(2, 1, 2, 9, share, chans),
+        (wout.astype(jnp.float32) * scale).reshape(2, 1, 2, 9, share, chans),
     )
 
 

time: 121 us -> 115 us (0.950)
  Pallas kernels: 115 us -> 110 us
  local copies, waits for them, and re-layouts: 5.19 us -> 0.8 us
  other arithmetic: 0 us -> 3.04 us
    pallas_call x1, Pallas kernels: 115 us -> 110 us  [on_device(): pl.pallas_call(functools.partial(kernel, dims), out_shape=(jax.ShapeDtype...]
    unnamed x2 -> x3, local copies, waits for them, and re-layouts: 5.19 us -> 0.8 us
    unnamed x0 -> x1, other arithmetic: none -> 3.04 us
where the time goes in v2:
time: 115 us
  Pallas kernels  110 us (96%)
  other arithmetic  3.04 us (3%)
    pallas_call x1, Pallas kernels, on_device(): pl.pallas_call(functools.partial(kernel, dims), out_shape=(jax.ShapeDtype...  110 us
    unnamed x1, other arithmetic  3.04 us

profile of v2, /device:TPU:4, one launch (start us, length us, event | category | flops | bytes accessed | tf_op | source)
XLA Modules:
  0.0 114.6 jit_solution(11302193406996157005)
XLA Ops:
  0.6 110.1 %shard_map.86 = (bf16[2,512,256]{2,1,0:T(8,128)(2,1)}, bf16[2,2,9,64,256]{4,3,2,1,0:T(8,128)(2,1)}) custom-call(s32[4,16]{1,0:T(4,128)} %slots.1, bf16[2,512,256]{2,1,0:T(8,128)(2,1)} %bitcast.18, bf16[2,4,512,256]{3,2,1,0:T(8,128)(2,1)} %bitcast.14, bf16[3,512,256]{2,1,0:T(8,128)(2,1)} %bitcast.17, bf16[2,4,512,256]{3,2,1,0:T(8,128)(2,1)} %bitcast.15, ...), custom_call_target="tpu_custom_call" | custom-call | tf_op jit(solution)/shard_map/pallas_call | solution.py:410
  110.7 0.0 copy-start
  110.7 3.0 %multiply_bitcast_fusion = f32[2,1,2,9,64,256]{5,4,3,2,1,0:T(8,128)} fusion(bf16[2,2,9,64,256]{4,3,2,1,0:T(8,128)(2,1)} %get-tuple-element.5), kind=kLoop, calls=%fused_computation | loop fusion | flops 1179648 | bytes 3538944
  113.8 0.0 copy-done
  113.8 0.8 copy.12
Async XLA Ops:
  110.7 3.1 %copy-start = (bf16[2,512,256]{2,1,0:T(8,128)(2,1)S(1)}, bf16[2,512,256]{2,1,0:T(8,128)(2,1)}, u32[]{:S(2)}) copy-start(bf16[2,512,256]{2,1,0:T(8,128)(2,1)} %get-tuple-element.4) | copy-start | bytes 1572868
